TPU v7x, 32 devices: a whole 2x2x4 slice. The times are simulated.
32 devices in a mesh: row: 8 (over z, x), col: 4 (over y, core).
Axes of the slice: x: 2, y: 2, z: 4, core: 2. Of those that a mesh axis runs over, the one named last changes fastest.
Arguments:
- obj_re: float32 [1024, 512], P('row', 'col'), may hold values from -6 to 6
- obj_im: float32 [1024, 512], P('row', 'col'), may hold values from -6 to 6
- probe_re: float32 [4, 256, 256], replicated, may hold values from -3 to 3
- probe_im: float32 [4, 256, 256], replicated, may hold values from -3 to 3
- amps: float32 [8, 4, 1, 256, 256], P('row', 'col'), may hold values from 0.2 to 4
- positions: int32 [8, 4, 1, 2], P('row', 'col'), may hold values from -128 to 896, as said below
Outputs:
- new_obj_re: float32 [1024, 512], P('row', 'col')
- new_obj_im: float32 [1024, 512], P('row', 'col')
- new_probe_re: float32 [4, 256, 256], replicated
- new_probe_im: float32 [4, 256, 256], replicated
Inputs may be any that keep to these rules, and one draw needn't show every extreme that they name: `positions`: each position's offsets are multiples of 64. A position stored at [i, j, p] has its row r with i * 128 - 256 // 2 <= r <= (i + 1) * 128 - 256 // 2 and its column c with j * 128 - 256 // 2 <= c <= (j + 1) * 128 - 256 // 2.
All inputs are finite; a program needn't handle non-finite values.
Results may differ from a plain program's by a relative error of at most 0.0055.
Values sent between devices are 32-bit elements; how exact they have to be, the bound alone decides.
No kernel may reach another device: no remote copies, remote signals or barrier semaphores. Data moves between devices by JAX's collectives and lax.ppermute only.
A program may use at most 64 MiB of HBM per device.

v0:
```python
import math
import jax
import jax.numpy as jnp
from jax import lax
from jax.sharding import PartitionSpec as P

ITERS = 3
amp_floor = 0.25
light_ratio = 0.1
mass_ratio = 0.1
probe_step = 6.0


def passed_along(array, axis, by):
    devices = lax.axis_size(axis)
    pairs = [(i, i + by) for i in range(devices) if 0 <= i + by < devices]
    return lax.ppermute(array, axis, pairs)


def with_halo(cells, sides, width):
    for axis, dim in sides:
        count = lax.axis_size(axis)
        ends = count - 1
        head = lax.slice_in_dim(cells, 0, width, axis=dim)
        tail = lax.slice_in_dim(cells, cells.shape[dim] - width, cells.shape[dim], axis=dim)
        cells = jnp.concatenate(
            [
                lax.ppermute(tail, axis, [(i, (i + 1) % count) for i in range(ends)]),
                cells,
                lax.ppermute(head, axis, [((i + 1) % count, i) for i in range(ends)]),
            ],
            axis=dim,
        )
    return cells


def make_tables(width, sign):
    index = jnp.arange(width, dtype=jnp.int32)
    turns = index[:, None] * index[None, :] % width
    angle = turns.astype(jnp.float32) * (2.0 * math.pi / width)
    real = (jnp.cos(angle) / math.sqrt(width)).astype(jnp.bfloat16)
    imag = (sign * jnp.sin(angle) / math.sqrt(width)).astype(jnp.bfloat16)
    right_pair = jnp.concatenate(
        [jnp.concatenate([real, imag], 1), jnp.concatenate([-imag, real], 1)], 0
    )
    return (right_pair, real, imag)


def transform(wave, table):
    right_pair, real, imag = table
    width = real.shape[0]
    half = jnp.einsum("mnc,cd->mnd", wave, right_pair, preferred_element_type=jnp.float32).astype(
        jnp.bfloat16
    )
    first = jnp.einsum("kn,mnd->mkd", real, half, preferred_element_type=jnp.float32)
    second = jnp.einsum("kn,mnd->mkd", imag, half, preferred_element_type=jnp.float32)
    return (first[..., :width] - second[..., width:], first[..., width:] + second[..., :width])


def one_view(window, probe_re, probe_im, view, forward, backward):
    win_re = window[0][None]
    win_im = window[1][None]
    psi = jnp.concatenate(
        [probe_re * win_re - probe_im * win_im, probe_re * win_im + probe_im * win_re], axis=2
    ).astype(jnp.bfloat16)
    spec_re, spec_im = transform(psi, forward)
    modulus = jnp.sqrt(jnp.sum(spec_re * spec_re + spec_im * spec_im, axis=0))
    factor = view / jnp.maximum(modulus, amp_floor) - 1.0
    change = jnp.concatenate([spec_re * factor, spec_im * factor], axis=2).astype(jnp.bfloat16)
    return transform(change, backward)


def place(buffer, piece, row_at, col_at):
    start = (jnp.int32(0), row_at, col_at)
    return lax.dynamic_update_slice(buffer, piece, start)


def send_rows(strip, offset):
    return passed_along(strip, "row", offset)


def send_cols(strip, offset):
    return passed_along(strip, "col", offset)


def fold_back(buffer, rows, cols, rim):
    middle = buffer[:, rim : rim + rows]
    from_below = send_rows(buffer[:, :rim], -1)
    from_above = send_rows(buffer[:, rim + rows :], 1)
    middle = middle.at[:, rows - rim :].add(from_below)
    middle = middle.at[:, :rim].add(from_above)
    core = middle[:, :, rim : rim + cols]
    from_right = send_cols(middle[:, :, :rim], -1)
    from_left = send_cols(middle[:, :, rim + cols :], 1)
    core = core.at[:, :, cols - rim :].add(from_right)
    return core.at[:, :, :rim].add(from_left)


def local(obj_re, obj_im, probe_re, probe_im, amps, positions):
    rows, cols = obj_re.shape
    modes, width = (probe_re.shape[0], probe_re.shape[1])
    rim = width // 2
    forward = make_tables(width, -1.0)
    backward = make_tables(width, 1.0)
    spots = positions[0, 0]
    views = amps[0, 0]
    my_row = lax.axis_index("row")
    my_col = lax.axis_index("col")
    row_base = my_row * rows - rim
    col_base = my_col * cols - rim
    local_rows = spots[:, 0] - row_base
    local_cols = spots[:, 1] - col_base
    wide_rows = rows + 2 * rim
    wide_cols = cols + 2 * rim
    power = jnp.sum(probe_re * probe_re + probe_im * probe_im, axis=0)
    light_buf = jnp.zeros((1, wide_rows, wide_cols), jnp.float32)
    slot = 0
    light_buf = place(light_buf, power[None], local_rows[slot], local_cols[slot])
    light = fold_back(light_buf, rows, cols, rim)[0]
    peak = lax.pmax(jnp.max(light), ("row", "col"))
    denom = light + light_ratio * peak
    state = jnp.stack([obj_re, obj_im])
    grad_re = jnp.zeros((modes, width, width), jnp.float32)
    grad_im = jnp.zeros((modes, width, width), jnp.float32)
    mass = jnp.zeros((width, width), jnp.float32)
    for step in range(ITERS):
        extended = with_halo(state, (("row", 1), ("col", 2)), rim)
        buffer = jnp.zeros((2, wide_rows, wide_cols), jnp.float32)
        last_pass = step == ITERS - 1
        slot = 0
        window = lax.dynamic_slice(
            extended, (jnp.int32(0), local_rows[slot], local_cols[slot]), (2, width, width)
        )
        exit_re, exit_im = one_view(window, probe_re, probe_im, views[slot], forward, backward)
        obj_grad = jnp.stack(
            [
                jnp.sum(probe_re * exit_re + probe_im * exit_im, axis=0),
                jnp.sum(probe_re * exit_im - probe_im * exit_re, axis=0),
            ]
        )
        buffer = place(buffer, obj_grad, local_rows[slot], local_cols[slot])
        if last_pass:
            win_re = window[0][None]
            win_im = window[1][None]
            grad_re = win_re * exit_re + win_im * exit_im
            grad_im = win_re * exit_im - win_im * exit_re
            mass = window[0] * window[0] + window[1] * window[1]
        state = state + fold_back(buffer, rows, cols, rim) / denom[None]
    pixels = width * width
    terms = jnp.concatenate(
        [grad_re.reshape(modes, pixels), grad_im.reshape(modes, pixels), mass.reshape(1, pixels)],
        axis=0,
    )
    probe_flat = jnp.concatenate(
        [probe_re.reshape(modes, pixels), probe_im.reshape(modes, pixels)], axis=0
    )
    summed = lax.psum(terms, ("row", "col"))
    scale = probe_step / (summed[2 * modes] + mass_ratio * jnp.mean(summed[2 * modes]))
    updated = probe_flat + summed[: 2 * modes] * scale[None]
    new_re = updated[:modes].reshape(modes, width, width)
    new_im = updated[modes:].reshape(modes, width, width)
    return (state[0], state[1], new_re, new_im)


def solution(mesh):
    placed = (
        P("row", "col"),
        P("row", "col"),
        P(),
        P(),
        P("row", "col", None, None, None),
        P("row", "col", None, None),
    )
    return jax.shard_map(
        local,
        mesh=mesh,
        in_specs=placed,
        out_specs=(P("row", "col"), P("row", "col"), P(), P()),
        check_vma=False,
    )
```

profile of v0, /device:TPU:0, one launch (start us, length us, event | category | flops | bytes accessed | tf_op | source)
XLA Modules:
  0.0 428.3 jit_solution(1866094221004445587)
XLA Ops:
  8.3 4.9 %collective-permute-start = (f32[2,128,128]{2,1,0:T(8,128)S(1)}, f32[2,128,128]{2,1,0:T(8,128)S(1)}, u32[]{:S(2)}, u32[]{:S(2)}) collective-permute-start(f32[2,128,128]{2,1,0:T(8,128)S(1)} %pad_maximum_fusion.11), channel_id=1, source_target_pairs={{0,4},{4,8},{8,12},{12,16},{16,20},{20,24},{24,28},{1,5},{5,9},{9,... | collective-permute-start | bytes 393224 | tf_op jit(solution)/shard_map/ppermute | solution.py:28
  16.1 3.9 collective-permute-done.1
  54.3 5.7 %collective-permute-start.9 = (f32[1,128,384]{2,1,0:T(8,128)}, f32[1,128,384]{2,1,0:T(8,128)}, u32[]{:S(2)}, u32[]{:S(2)}) collective-permute-start(f32[1,128,384]{2,1,0:T(8,128)} %get-tuple-element.356), channel_id=1, source_target_pairs={{0,4},{4,8},{8,12},{12,16},{16,20},{20,24},{24,28},{1,5},{5,9},{9,... | collective-permute-start | bytes 589832 | tf_op jit(solution)/shard_map/ppermute | solution.py:17
  67.0 4.5 %dynamic_update_slice.12 = f32[2,384,384]{2,1,0:T(8,128)} dynamic-update-slice(f32[2,384,384]{2,1,0:T(8,128)} %broadcast.616.clone, f32[2,256,256]{2,1,0:T(8,128)} %copy.48, s32[]{:T(128)} %constant.548.clone.1, s32[]{:T(128)S(6)} %select_n.65, s32[]{:T(128)S(6)} %select_n.66) | dynamic-update-slice | bytes 1048580 | tf_op jit(solution)/shard_map/dynamic_update_slice | solution.py:75
  74.9 5.5 %collective-permute-start.5 = (f32[2,128,384]{2,1,0:T(8,128)}, f32[2,128,384]{2,1,0:T(8,128)}, u32[]{:S(2)}, u32[]{:S(2)}) collective-permute-start(f32[2,128,384]{2,1,0:T(8,128)} %get-tuple-element.354), channel_id=1, source_target_pairs={{0,4},{4,8},{8,12},{12,16},{16,20},{20,24},{24,28},{1,5},{5,9},{9,... | collective-permute-start | bytes 1179656 | tf_op jit(solution)/shard_map/ppermute | solution.py:17
  82.9 3.8 collective-permute-start.11
  88.2 46.3 %pmax.7 = f32[]{:T(128)} all-reduce(f32[]{:T(128)} %fusion.146), channel_id=1, replica_groups=mesh['row'=8,'col'=4] {'row','col'}, use_global_device_ids=true, to_apply=%region_5.6 | all-reduce | flops 1 | bytes 8 | tf_op jit(solution)/shard_map/pmax | solution.py:120
  142.7 4.2 collective-permute-start.12
  150.8 4.4 %collective-permute-done.13 = f32[2,128,128]{2,1,0:T(8,128)S(1)} collective-permute-done((f32[2,128,128]{2,1,0:T(8,128)S(1)}, f32[2,128,128]{2,1,0:T(8,128)S(1)}, u32[]{:S(2)}, u32[]{:S(2)}) %collective-permute-start.13) | collective-permute-done | bytes 131104 | tf_op jit(solution)/shard_map/ppermute | solution.py:30
  158.6 3.8 collective-permute-done.15
  174.1 5.9 %dynamic_update_slice.14 = f32[2,384,384]{2,1,0:T(8,128)S(1)} dynamic-update-slice(f32[2,384,384]{2,1,0:T(8,128)S(1)} %broadcast.616.clone.1, f32[2,256,256]{2,1,0:T(8,128)} %copy.58, s32[]{:T(128)} %constant.548.clone.1, s32[]{:T(128)S(6)} %select_n.65, s32[]{:T(128)S(6)} %select_n.66) | dynamic-update-slice | bytes 1048580 | tf_op jit(solution)/shard_map/dynamic_update_slice | solution.py:75
  181.5 5.5 %collective-permute-start.17 = (f32[2,128,384]{2,1,0:T(8,128)S(1)}, f32[2,128,384]{2,1,0:T(8,128)S(1)}, u32[]{:S(2)}, u32[]{:S(2)}) collective-permute-start(f32[2,128,384]{2,1,0:T(8,128)S(1)} %get-tuple-element.352), channel_id=1, source_target_pairs={{0,4},{4,8},{8,12},{12,16},{16,20},{20,24},{24,28},{1,5},{5,9},{9,... | collective-permute-start | bytes 1179656 | tf_op jit(solution)/shard_map/ppermute | solution.py:17
  186.9 3.8 collective-permute-done.16
  190.7 12.4 %collective-permute-done.17 = f32[2,128,384]{2,1,0:T(8,128)S(1)} collective-permute-done((f32[2,128,384]{2,1,0:T(8,128)S(1)}, f32[2,128,384]{2,1,0:T(8,128)S(1)}, u32[]{:S(2)}, u32[]{:S(2)}) %collective-permute-start.17) | collective-permute-done | bytes 393248 | tf_op jit(solution)/shard_map/ppermute | solution.py:17
  204.5 3.3 collective-permute-start.19
  208.9 4.1 collective-permute-start.20
  215.5 4.4 %collective-permute-done.21 = f32[2,128,128]{2,1,0:T(8,128)S(1)} collective-permute-done((f32[2,128,128]{2,1,0:T(8,128)S(1)}, f32[2,128,128]{2,1,0:T(8,128)S(1)}, u32[]{:S(2)}, u32[]{:S(2)}) %collective-permute-start.21) | collective-permute-done | bytes 131104 | tf_op jit(solution)/shard_map/ppermute | solution.py:30
  224.6 5.7 %collective-permute-done.23 = f32[2,384,128]{2,1,0:T(8,128)S(1)} collective-permute-done((f32[2,384,128]{2,1,0:T(8,128)S(1)}, f32[2,384,128]{2,1,0:T(8,128)S(1)}, u32[]{:S(2)}, u32[]{:S(2)}) %collective-permute-start.23) | collective-permute-done | bytes 393248 | tf_op jit(solution)/shard_map/ppermute | solution.py:30
  245.7 5.9 %dynamic_update_slice.15 = f32[2,384,384]{2,1,0:T(8,128)S(1)} dynamic-update-slice(f32[2,384,384]{2,1,0:T(8,128)S(1)} %broadcast.616, f32[2,256,256]{2,1,0:T(8,128)} %pad_maximum_fusion.7, s32[]{:T(128)} %constant.548.clone.1, s32[]{:T(128)S(6)} %select_n.65, s32[]{:T(128)S(6)} %select_n.66) | dynamic-update-slice | bytes 1048580 | tf_op jit(solution)/shard_map/dynamic_update_slice | solution.py:75
  253.9 5.5 %collective-permute-start.25 = (f32[2,128,384]{2,1,0:T(8,128)}, f32[2,128,384]{2,1,0:T(8,128)}, u32[]{:S(2)}, u32[]{:S(2)}) collective-permute-start(f32[2,128,384]{2,1,0:T(8,128)} %get-tuple-element.350), channel_id=1, source_target_pairs={{0,4},{4,8},{8,12},{12,16},{16,20},{20,24},{24,28},{1,5},{5,9},{9,... | collective-permute-start | bytes 1179656 | tf_op jit(solution)/shard_map/ppermute | solution.py:17
  259.4 3.9 pad_maximum_fusion
  263.4 10.7 %collective-permute-done.25 = f32[2,128,384]{2,1,0:T(8,128)} collective-permute-done((f32[2,128,384]{2,1,0:T(8,128)}, f32[2,128,384]{2,1,0:T(8,128)}, u32[]{:S(2)}, u32[]{:S(2)}) %collective-permute-start.25) | collective-permute-done | bytes 393248 | tf_op jit(solution)/shard_map/ppermute | solution.py:17
  276.6 6.9 %collective-permute-start.27 = (f32[2,128,128]{2,1,0:T(8,128)S(1)}, f32[2,128,128]{2,1,0:T(8,128)S(1)}, u32[]{:S(2)}, u32[]{:S(2)}) collective-permute-start(f32[2,128,128]{2,1,0:T(8,128)S(1)} %get-tuple-element.365), channel_id=1, source_target_pairs={{0,1},{1,2},{2,3},{4,5},{5,6},{6,7},{8,9},{9,10},{10,11},{12,13},{... | collective-permute-start | bytes 393224 | tf_op jit(solution)/shard_map/ppermute | solution.py:17
  286.6 124.2 %all-reduce.2.cloned.1.call-done = f32[9,65536]{1,0:T(8,128)} async-done(((f32[9,65536]{1,0:T(8,128)}), f32[9,65536]{1,0:T(8,128)}) %all-reduce.2.cloned.1.call-update) | async-done | bytes 2359312 | tf_op jit(solution)/shard_map/psum | solution.py:157
  (193 shorter events, 121.3 us)
Async XLA Ops:
  7.2 403.6 %all-reduce.2.cloned.1.call-start = ((), (), s32[]{:S(2)}) async-start(), calls=%async_computation | async-start | bytes 8388608 | tf_op jit(solution)/shard_map/psum | solution.py:157
  8.3 7.8 %collective-permute-start = (f32[2,128,128]{2,1,0:T(8,128)S(1)}, f32[2,128,128]{2,1,0:T(8,128)S(1)}, u32[]{:S(2)}, u32[]{:S(2)}) collective-permute-start(f32[2,128,128]{2,1,0:T(8,128)S(1)} %pad_maximum_fusion.11), channel_id=1, source_target_pairs={{0,4},{4,8},{8,12},{12,16},{16,20},{20,24},{24,28},{1,5},{5,9},{9,... | collective-permute-start | bytes 393224 | tf_op jit(solution)/shard_map/ppermute | solution.py:28
  13.1 6.9 %collective-permute-start.1 = (f32[2,128,128]{2,1,0:T(8,128)S(1)}, f32[2,128,128]{2,1,0:T(8,128)S(1)}, u32[]{:S(2)}, u32[]{:S(2)}) collective-permute-start(f32[2,128,128]{2,1,0:T(8,128)S(1)} %pad_maximum_fusion.11), channel_id=1, source_target_pairs={{4,0},{8,4},{12,8},{16,12},{20,16},{24,20},{28,24},{5,1},{9,5},{13... | collective-permute-start | bytes 393224 | tf_op jit(solution)/shard_map/ppermute | solution.py:30
  21.7 12.4 %collective-permute-start.2 = (f32[2,384,128]{2,1,0:T(8,128)}, f32[2,384,128]{2,1,0:T(8,128)}, u32[]{:S(2)}, u32[]{:S(2)}) collective-permute-start(f32[2,384,128]{2,1,0:T(8,128)} %pad_maximum_fusion.8), channel_id=1, source_target_pairs={{0,1},{1,2},{2,3},{4,5},{5,6},{6,7},{8,9},{9,10},{10,11},{12,13},{... | collective-permute-start | bytes 1179656 | tf_op jit(solution)/shard_map/ppermute | solution.py:28
  23.7 10.4 %collective-permute-start.3 = (f32[2,384,128]{2,1,0:T(8,128)}, f32[2,384,128]{2,1,0:T(8,128)}, u32[]{:S(2)}, u32[]{:S(2)}) collective-permute-start(f32[2,384,128]{2,1,0:T(8,128)} %pad_maximum_fusion.8), channel_id=1, source_target_pairs={{1,0},{2,1},{3,2},{5,4},{6,5},{7,6},{9,8},{10,9},{11,10},{13,12},{... | collective-permute-start | bytes 1179656 | tf_op jit(solution)/shard_map/ppermute | solution.py:30
  53.0 27.5 %collective-permute-start.8 = (f32[1,128,384]{2,1,0:T(8,128)}, f32[1,128,384]{2,1,0:T(8,128)}, u32[]{:S(2)}, u32[]{:S(2)}) collective-permute-start(f32[1,128,384]{2,1,0:T(8,128)} %get-tuple-element.355), channel_id=1, source_target_pairs={{4,0},{8,4},{12,8},{16,12},{20,16},{24,20},{28,24},{5,1},{9,5},{13... | collective-permute-start | bytes 589832 | tf_op jit(solution)/shard_map/ppermute | solution.py:17
  54.3 26.2 %collective-permute-start.9 = (f32[1,128,384]{2,1,0:T(8,128)}, f32[1,128,384]{2,1,0:T(8,128)}, u32[]{:S(2)}, u32[]{:S(2)}) collective-permute-start(f32[1,128,384]{2,1,0:T(8,128)} %get-tuple-element.356), channel_id=1, source_target_pairs={{0,4},{4,8},{8,12},{12,16},{16,20},{20,24},{24,28},{1,5},{5,9},{9,... | collective-permute-start | bytes 589832 | tf_op jit(solution)/shard_map/ppermute | solution.py:17
  73.6 61.6 %collective-permute-start.4 = (f32[2,128,384]{2,1,0:T(8,128)}, f32[2,128,384]{2,1,0:T(8,128)}, u32[]{:S(2)}, u32[]{:S(2)}) collective-permute-start(f32[2,128,384]{2,1,0:T(8,128)} %get-tuple-element.353), channel_id=1, source_target_pairs={{4,0},{8,4},{12,8},{16,12},{20,16},{24,20},{28,24},{5,1},{9,5},{13... | collective-permute-start | bytes 1179656 | tf_op jit(solution)/shard_map/ppermute | solution.py:17
  74.9 60.3 %collective-permute-start.5 = (f32[2,128,384]{2,1,0:T(8,128)}, f32[2,128,384]{2,1,0:T(8,128)}, u32[]{:S(2)}, u32[]{:S(2)}) collective-permute-start(f32[2,128,384]{2,1,0:T(8,128)} %get-tuple-element.354), channel_id=1, source_target_pairs={{0,4},{4,8},{8,12},{12,16},{16,20},{20,24},{24,28},{1,5},{5,9},{9,... | collective-permute-start | bytes 1179656 | tf_op jit(solution)/shard_map/ppermute | solution.py:17
  81.6 5.1 %collective-permute-start.10 = (f32[1,128,128]{2,1,0:T(8,128)S(1)}, f32[1,128,128]{2,1,0:T(8,128)S(1)}, u32[]{:S(2)}, u32[]{:S(2)}) collective-permute-start(f32[1,128,128]{2,1,0:T(8,128)S(1)} %get-tuple-element.370), channel_id=1, source_target_pairs={{1,0},{2,1},{3,2},{5,4},{6,5},{7,6},{9,8},{10,9},{11,10},{13,12},{... | collective-permute-start | bytes 196616 | tf_op jit(solution)/shard_map/ppermute | solution.py:17
  136.5 5.2 %collective-permute-start.6 = (f32[2,128,128]{2,1,0:T(8,128)S(1)}, f32[2,128,128]{2,1,0:T(8,128)S(1)}, u32[]{:S(2)}, u32[]{:S(2)}) collective-permute-start(f32[2,128,128]{2,1,0:T(8,128)S(1)} %get-tuple-element.368), channel_id=1, source_target_pairs={{1,0},{2,1},{3,2},{5,4},{6,5},{7,6},{9,8},{10,9},{11,10},{13,12},{... | collective-permute-start | bytes 393224 | tf_op jit(solution)/shard_map/ppermute | solution.py:17
  142.7 8.1 %collective-permute-start.12 = (f32[2,128,128]{2,1,0:T(8,128)S(1)}, f32[2,128,128]{2,1,0:T(8,128)S(1)}, u32[]{:S(2)}, u32[]{:S(2)}) collective-permute-start(f32[2,128,128]{2,1,0:T(8,128)S(1)} %fusion.63), channel_id=1, source_target_pairs={{0,4},{4,8},{8,12},{12,16},{16,20},{20,24},{24,28},{1,5},{5,9},{9,... | collective-permute-start | bytes 393224 | tf_op jit(solution)/shard_map/ppermute | solution.py:28
  146.9 8.2 %collective-permute-start.13 = (f32[2,128,128]{2,1,0:T(8,128)S(1)}, f32[2,128,128]{2,1,0:T(8,128)S(1)}, u32[]{:S(2)}, u32[]{:S(2)}) collective-permute-start(f32[2,128,128]{2,1,0:T(8,128)S(1)} %fusion.63), channel_id=1, source_target_pairs={{4,0},{8,4},{12,8},{16,12},{20,16},{24,20},{28,24},{5,1},{9,5},{13... | collective-permute-start | bytes 393224 | tf_op jit(solution)/shard_map/ppermute | solution.py:30
  157.2 5.1 %collective-permute-start.15 = (f32[2,384,128]{2,1,0:T(8,128)S(1)}, f32[2,384,128]{2,1,0:T(8,128)S(1)}, u32[]{:S(2)}, u32[]{:S(2)}) collective-permute-start(f32[2,384,128]{2,1,0:T(8,128)S(1)} %pad_maximum_fusion.9), channel_id=1, source_target_pairs={{1,0},{2,1},{3,2},{5,4},{6,5},{7,6},{9,8},{10,9},{11,10},{13,12},{... | collective-permute-start | bytes 1179656 | tf_op jit(solution)/shard_map/ppermute | solution.py:30
  180.2 10.6 %collective-permute-start.16 = (f32[2,128,384]{2,1,0:T(8,128)S(1)}, f32[2,128,384]{2,1,0:T(8,128)S(1)}, u32[]{:S(2)}, u32[]{:S(2)}) collective-permute-start(f32[2,128,384]{2,1,0:T(8,128)S(1)} %get-tuple-element.351), channel_id=1, source_target_pairs={{4,0},{8,4},{12,8},{16,12},{20,16},{24,20},{28,24},{5,1},{9,5},{13... | collective-permute-start | bytes 1179656 | tf_op jit(solution)/shard_map/ppermute | solution.py:17
  181.5 21.7 %collective-permute-start.17 = (f32[2,128,384]{2,1,0:T(8,128)S(1)}, f32[2,128,384]{2,1,0:T(8,128)S(1)}, u32[]{:S(2)}, u32[]{:S(2)}) collective-permute-start(f32[2,128,384]{2,1,0:T(8,128)S(1)} %get-tuple-element.352), channel_id=1, source_target_pairs={{0,4},{4,8},{8,12},{12,16},{16,20},{20,24},{24,28},{1,5},{5,9},{9,... | collective-permute-start | bytes 1179656 | tf_op jit(solution)/shard_map/ppermute | solution.py:17
  208.9 6.6 %collective-permute-start.20 = (f32[2,128,128]{2,1,0:T(8,128)S(1)}, f32[2,128,128]{2,1,0:T(8,128)S(1)}, u32[]{:S(2)}, u32[]{:S(2)}) collective-permute-start(f32[2,128,128]{2,1,0:T(8,128)S(1)} %fusion.60), channel_id=1, source_target_pairs={{0,4},{4,8},{8,12},{12,16},{16,20},{20,24},{24,28},{1,5},{5,9},{9,... | collective-permute-start | bytes 393224 | tf_op jit(solution)/shard_map/ppermute | solution.py:28
  213.0 6.9 %collective-permute-start.21 = (f32[2,128,128]{2,1,0:T(8,128)S(1)}, f32[2,128,128]{2,1,0:T(8,128)S(1)}, u32[]{:S(2)}, u32[]{:S(2)}) collective-permute-start(f32[2,128,128]{2,1,0:T(8,128)S(1)} %fusion.60), channel_id=1, source_target_pairs={{4,0},{8,4},{12,8},{16,12},{20,16},{24,20},{28,24},{5,1},{9,5},{13... | collective-permute-start | bytes 393224 | tf_op jit(solution)/shard_map/ppermute | solution.py:30
  219.9 4.7 %collective-permute-start.22 = (f32[2,384,128]{2,1,0:T(8,128)S(1)}, f32[2,384,128]{2,1,0:T(8,128)S(1)}, u32[]{:S(2)}, u32[]{:S(2)}) collective-permute-start(f32[2,384,128]{2,1,0:T(8,128)S(1)} %pad_maximum_fusion.10), channel_id=1, source_target_pairs={{0,1},{1,2},{2,3},{4,5},{5,6},{6,7},{8,9},{9,10},{10,11},{12,13},{... | collective-permute-start | bytes 1179656 | tf_op jit(solution)/shard_map/ppermute | solution.py:28
  223.1 7.2 %collective-permute-start.23 = (f32[2,384,128]{2,1,0:T(8,128)S(1)}, f32[2,384,128]{2,1,0:T(8,128)S(1)}, u32[]{:S(2)}, u32[]{:S(2)}) collective-permute-start(f32[2,384,128]{2,1,0:T(8,128)S(1)} %pad_maximum_fusion.10), channel_id=1, source_target_pairs={{1,0},{2,1},{3,2},{5,4},{6,5},{7,6},{9,8},{10,9},{11,10},{13,12},{... | collective-permute-start | bytes 1179656 | tf_op jit(solution)/shard_map/ppermute | solution.py:30
  252.6 10.8 %collective-permute-start.24 = (f32[2,128,384]{2,1,0:T(8,128)}, f32[2,128,384]{2,1,0:T(8,128)}, u32[]{:S(2)}, u32[]{:S(2)}) collective-permute-start(f32[2,128,384]{2,1,0:T(8,128)} %get-tuple-element.349), channel_id=1, source_target_pairs={{4,0},{8,4},{12,8},{16,12},{20,16},{24,20},{28,24},{5,1},{9,5},{13... | collective-permute-start | bytes 1179656 | tf_op jit(solution)/shard_map/ppermute | solution.py:17
  253.9 20.2 %collective-permute-start.25 = (f32[2,128,384]{2,1,0:T(8,128)}, f32[2,128,384]{2,1,0:T(8,128)}, u32[]{:S(2)}, u32[]{:S(2)}) collective-permute-start(f32[2,128,384]{2,1,0:T(8,128)} %get-tuple-element.350), channel_id=1, source_target_pairs={{0,4},{4,8},{8,12},{12,16},{16,20},{20,24},{24,28},{1,5},{5,9},{9,... | collective-permute-start | bytes 1179656 | tf_op jit(solution)/shard_map/ppermute | solution.py:17
  275.3 10.6 %collective-permute-start.26 = (f32[2,128,128]{2,1,0:T(8,128)S(1)}, f32[2,128,128]{2,1,0:T(8,128)S(1)}, u32[]{:S(2)}, u32[]{:S(2)}) collective-permute-start(f32[2,128,128]{2,1,0:T(8,128)S(1)} %get-tuple-element.364), channel_id=1, source_target_pairs={{1,0},{2,1},{3,2},{5,4},{6,5},{7,6},{9,8},{10,9},{11,10},{13,12},{... | collective-permute-start | bytes 393224 | tf_op jit(solution)/shard_map/ppermute | solution.py:17
  276.6 9.3 %collective-permute-start.27 = (f32[2,128,128]{2,1,0:T(8,128)S(1)}, f32[2,128,128]{2,1,0:T(8,128)S(1)}, u32[]{:S(2)}, u32[]{:S(2)}) collective-permute-start(f32[2,128,128]{2,1,0:T(8,128)S(1)} %get-tuple-element.365), channel_id=1, source_target_pairs={{0,1},{1,2},{2,3},{4,5},{5,6},{6,7},{8,9},{9,10},{10,11},{12,13},{... | collective-permute-start | bytes 393224 | tf_op jit(solution)/shard_map/ppermute | solution.py:17
  (36 other events, 250.2 us)
Sparse Core Ops, SparseCore 0:
  263.5 147.2 all-reduce.1
where the time goes:
time: 434 us; the launch traced here: 428 us
  waiting for transfers between devices  179 us (41%)
  starting transfers between devices  78 us (18%)
  blocking collectives  46.3 us (11%)
  local copies, waits for them, and re-layouts  44.9 us (10%)
  other arithmetic  38.7 us (9%)
  matrix products  23.7 us (5%)
  between operations  17.9 us (4%)
    psum x1, waiting for transfers between devices, local(): summed = lax.psum(terms, ('row', 'col'))  124 us
    ppermute x16, starting transfers between devices, passed_along(): return lax.ppermute(array, axis, pairs)  49.6 us
    pmax x1, blocking collectives, local(): peak = lax.pmax(jnp.max(light), ('row', 'col'))  46.3 us
    ppermute x16, waiting for transfers between devices, passed_along(): return lax.ppermute(array, axis, pairs)  28.8 us
    ppermute x6, waiting for transfers between devices, with_halo(): lax.ppermute(head, axis, [((i + 1) % count, i) for i in range(ends)])  22.1 us
    ppermute x6, starting transfers between devices, with_halo(): lax.ppermute(tail, axis, [(i, (i + 1) % count) for i in range(ends)])  20.4 us
    dynamic_update_slice x4, local copies, waits for them, and re-layouts, place(): return lax.dynamic_update_slice(buffer, piece, start)  19 us
    unnamed x72, local copies, waits for them, and re-layouts  13.4 us
  transfers between devices with their start and end apart: 29, of which 14 were waited for; matrix products, arithmetic and copies ran while one was open for 8% of the time, Pallas kernels for 0%

commit v1 on v0

--- a/solution.py
+++ b/solution.py
@@ -1,3 +1,4 @@
+import functools
 import math
 import jax
 import jax.numpy as jnp
@@ -9,6 +10,15 @@
 light_ratio = 0.1
 mass_ratio = 0.1
 probe_step = 6.0
+
+
+def scenes_watch(target, peer_axis, shard_axis):
+    for d in (peer_axis, shard_axis):
+        target = lax.psum(target, d)
+    return target
+
+
+_divide_gates = functools.partial(scenes_watch, peer_axis="row", shard_axis="col")
 
 
 def passed_along(array, axis, by):
@@ -154,7 +164,7 @@
     probe_flat = jnp.concatenate(
         [probe_re.reshape(modes, pixels), probe_im.reshape(modes, pixels)], axis=0
     )
-    summed = lax.psum(terms, ("row", "col"))
+    summed = _divide_gates(terms)
     scale = probe_step / (summed[2 * modes] + mass_ratio * jnp.mean(summed[2 * modes]))
     updated = probe_flat + summed[: 2 * modes] * scale[None]
     new_re = updated[:modes].reshape(modes, width, width)

time: 434 us -> 525 us (1.21)
  waiting for transfers between devices: 179 us -> 277 us
    psum x1 -> x2, waiting for transfers between devices: 124 us -> 233 us  [scenes_watch(): target = lax.psum(target, d)]
    ppermute x16, waiting for transfers between devices: 28.8 us -> 18.1 us  [passed_along(): return lax.ppermute(array, axis, pairs)]
    unnamed x72 -> x70, local copies, waits for them, and re-layouts: 13.4 us -> 11.5 us
  transfers between devices with their start and end apart: 29 -> 30, of which waited for: 14 -> 14; matrix products, arithmetic and copies ran while one was open for 8% -> 7% of each run, Pallas kernels for 0% -> 0%
where the time goes in v1:
time: 525 us; the launch traced here: 519 us
  waiting for transfers between devices  277 us (53%)
  starting transfers between devices  74.2 us (14%)
  blocking collectives  46.3 us (9%)
  local copies, waits for them, and re-layouts  43 us (8%)
  other arithmetic  37.4 us (7%)
  matrix products  23.7 us (5%)
  between operations  17.9 us (3%)
    psum x2, waiting for transfers between devices, scenes_watch(): target = lax.psum(target, d)  233 us
    pmax x1, blocking collectives, local(): peak = lax.pmax(jnp.max(light), ('row', 'col'))  46.3 us
    ppermute x16, starting transfers between devices, passed_along(): return lax.ppermute(array, axis, pairs)  45.5 us
    ppermute x6, waiting for transfers between devices, with_halo(): lax.ppermute(head, axis, [((i + 1) % count, i) for i in range(ends)])  22.1 us
    ppermute x6, starting transfers between devices, with_halo(): lax.ppermute(tail, axis, [(i, (i + 1) % count) for i in range(ends)])  20.4 us
    dynamic_update_slice x4, local copies, waits for them, and re-layouts, place(): return lax.dynamic_update_slice(buffer, piece, start)  19 us
    ppermute x16, waiting for transfers between devices, passed_along(): return lax.ppermute(array, axis, pairs)  18.1 us
    unnamed x70, local copies, waits for them, and re-layouts  11.5 us
  transfers between devices with their start and end apart: 30, of which 14 were waited for; matrix products, arithmetic and copies ran while one was open for 7% of the time, Pallas kernels for 0%

profile of v1, /device:TPU:0, one launch (start us, length us, event | category | flops | bytes accessed | tf_op | source)
XLA Modules:
  0.0 519.0 jit_solution(1071666385682035322)
XLA Ops:
  8.3 4.9 collective-permute-start
  16.1 3.9 collective-permute-done.1
  54.3 5.7 %collective-permute-start.9 = (f32[1,128,384]{2,1,0:T(8,128)}, f32[1,128,384]{2,1,0:T(8,128)}, u32[]{:S(2)}, u32[]{:S(2)}) collective-permute-start(f32[1,128,384]{2,1,0:T(8,128)} %get-tuple-element.356), channel_id=1, source_target_pairs={{0,4},{4,8},{8,12},{12,16},{16,20},{20,24},{24,28},{1,5},{5,9},{9,... | collective-permute-start | bytes 589832 | tf_op jit(solution)/shard_map/ppermute | solution.py:27
  60.0 3.0 add_reduce_fusion.5
  67.0 4.6 dynamic_update_slice.12
  75.0 5.5 %collective-permute-start.5 = (f32[2,128,384]{2,1,0:T(8,128)}, f32[2,128,384]{2,1,0:T(8,128)}, u32[]{:S(2)}, u32[]{:S(2)}) collective-permute-start(f32[2,128,384]{2,1,0:T(8,128)} %get-tuple-element.354), channel_id=1, source_target_pairs={{0,4},{4,8},{8,12},{12,16},{16,20},{20,24},{24,28},{1,5},{5,9},{9,... | collective-permute-start | bytes 1179656 | tf_op jit(solution)/shard_map/ppermute | solution.py:27
  83.0 3.8 collective-permute-start.11
  88.3 46.3 %pmax.7 = f32[]{:T(128)} all-reduce(f32[]{:T(128)} %fusion.146), channel_id=1, replica_groups=mesh['row'=8,'col'=4] {'row','col'}, use_global_device_ids=true, to_apply=%region_5.6 | all-reduce | flops 1 | bytes 8 | tf_op jit(solution)/shard_map/pmax | solution.py:130
  142.8 4.2 collective-permute-start.12
  150.9 4.4 collective-permute-done.13
  158.6 3.7 collective-permute-done.15
  174.2 5.9 %dynamic_update_slice.14 = f32[2,384,384]{2,1,0:T(8,128)S(1)} dynamic-update-slice(f32[2,384,384]{2,1,0:T(8,128)S(1)} %broadcast.616.clone.1, f32[2,256,256]{2,1,0:T(8,128)} %copy.58, s32[]{:T(128)} %constant.548.clone.1, s32[]{:T(128)S(6)} %select_n.65, s32[]{:T(128)S(6)} %select_n.66) | dynamic-update-slice | bytes 1048580 | tf_op jit(solution)/shard_map/dynamic_update_slice | solution.py:85
  181.5 5.5 %collective-permute-start.17 = (f32[2,128,384]{2,1,0:T(8,128)S(1)}, f32[2,128,384]{2,1,0:T(8,128)S(1)}, u32[]{:S(2)}, u32[]{:S(2)}) collective-permute-start(f32[2,128,384]{2,1,0:T(8,128)S(1)} %get-tuple-element.352), channel_id=1, source_target_pairs={{0,4},{4,8},{8,12},{12,16},{16,20},{20,24},{24,28},{1,5},{5,9},{9,... | collective-permute-start | bytes 1179656 | tf_op jit(solution)/shard_map/ppermute | solution.py:27
  187.0 3.8 collective-permute-done.16
  190.8 12.4 %collective-permute-done.17 = f32[2,128,384]{2,1,0:T(8,128)S(1)} collective-permute-done((f32[2,128,384]{2,1,0:T(8,128)S(1)}, f32[2,128,384]{2,1,0:T(8,128)S(1)}, u32[]{:S(2)}, u32[]{:S(2)}) %collective-permute-start.17) | collective-permute-done | bytes 393248 | tf_op jit(solution)/shard_map/ppermute | solution.py:27
  204.6 3.3 collective-permute-start.19
  208.9 4.1 collective-permute-start.20
  215.5 4.4 collective-permute-done.21
  219.9 3.2 collective-permute-start.22
  224.6 5.7 %collective-permute-done.23 = f32[2,384,128]{2,1,0:T(8,128)S(1)} collective-permute-done((f32[2,384,128]{2,1,0:T(8,128)S(1)}, f32[2,384,128]{2,1,0:T(8,128)S(1)}, u32[]{:S(2)}, u32[]{:S(2)}) %collective-permute-start.23) | collective-permute-done | bytes 393248 | tf_op jit(solution)/shard_map/ppermute | solution.py:40
  246.8 5.9 %dynamic_update_slice.15 = f32[2,384,384]{2,1,0:T(8,128)S(1)} dynamic-update-slice(f32[2,384,384]{2,1,0:T(8,128)S(1)} %broadcast.616, f32[2,256,256]{2,1,0:T(8,128)} %pad_maximum_fusion.7, s32[]{:T(128)} %constant.548.clone.1, s32[]{:T(128)S(6)} %select_n.65, s32[]{:T(128)S(6)} %select_n.66) | dynamic-update-slice | bytes 1048580 | tf_op jit(solution)/shard_map/dynamic_update_slice | solution.py:85
  255.0 5.3 %collective-permute-start.25 = (f32[2,128,384]{2,1,0:T(8,128)}, f32[2,128,384]{2,1,0:T(8,128)}, u32[]{:S(2)}, u32[]{:S(2)}) collective-permute-start(f32[2,128,384]{2,1,0:T(8,128)} %get-tuple-element.350), channel_id=1, source_target_pairs={{0,4},{4,8},{8,12},{12,16},{16,20},{20,24},{24,28},{1,5},{5,9},{9,... | collective-permute-start | bytes 1179656 | tf_op jit(solution)/shard_map/ppermute | solution.py:27
  260.3 154.3 %all-reduce.3.cloned.1.call-done = f32[9,65536]{1,0:T(8,128)} async-done(((f32[9,65536]{1,0:T(8,128)}), f32[9,65536]{1,0:T(8,128)}) %all-reduce.3.cloned.1.call-update) | async-done | bytes 2359312 | tf_op jit(solution)/shard_map/psum | solution.py:17
  423.3 78.2 %all-reduce.5.cloned.1.call-done = f32[9,65536]{1,0:T(8,128)} async-done(((f32[9,65536]{1,0:T(8,128)}), f32[9,65536]{1,0:T(8,128)}) %all-reduce.5.cloned.1.call-update) | async-done | bytes 2359312 | tf_op jit(solution)/shard_map/psum | solution.py:17
  (194 shorter events, 119.1 us)
Async XLA Ops:
  7.2 407.4 %all-reduce.3.cloned.1.call-start = ((), (), s32[]{:S(2)}) async-start(), calls=%async_computation | async-start | bytes 8388608 | tf_op jit(solution)/shard_map/psum | solution.py:17
  8.3 7.8 %collective-permute-start = (f32[2,128,128]{2,1,0:T(8,128)S(1)}, f32[2,128,128]{2,1,0:T(8,128)S(1)}, u32[]{:S(2)}, u32[]{:S(2)}) collective-permute-start(f32[2,128,128]{2,1,0:T(8,128)S(1)} %pad_maximum_fusion.11), channel_id=1, source_target_pairs={{0,4},{4,8},{8,12},{12,16},{16,20},{20,24},{24,28},{1,5},{5,9},{9,... | collective-permute-start | bytes 393224 | tf_op jit(solution)/shard_map/ppermute | solution.py:38
  13.1 6.9 %collective-permute-start.1 = (f32[2,128,128]{2,1,0:T(8,128)S(1)}, f32[2,128,128]{2,1,0:T(8,128)S(1)}, u32[]{:S(2)}, u32[]{:S(2)}) collective-permute-start(f32[2,128,128]{2,1,0:T(8,128)S(1)} %pad_maximum_fusion.11), channel_id=1, source_target_pairs={{4,0},{8,4},{12,8},{16,12},{20,16},{24,20},{28,24},{5,1},{9,5},{13... | collective-permute-start | bytes 393224 | tf_op jit(solution)/shard_map/ppermute | solution.py:40
  21.7 12.4 %collective-permute-start.2 = (f32[2,384,128]{2,1,0:T(8,128)}, f32[2,384,128]{2,1,0:T(8,128)}, u32[]{:S(2)}, u32[]{:S(2)}) collective-permute-start(f32[2,384,128]{2,1,0:T(8,128)} %pad_maximum_fusion.8), channel_id=1, source_target_pairs={{0,1},{1,2},{2,3},{4,5},{5,6},{6,7},{8,9},{9,10},{10,11},{12,13},{... | collective-permute-start | bytes 1179656 | tf_op jit(solution)/shard_map/ppermute | solution.py:38
  23.7 10.4 %collective-permute-start.3 = (f32[2,384,128]{2,1,0:T(8,128)}, f32[2,384,128]{2,1,0:T(8,128)}, u32[]{:S(2)}, u32[]{:S(2)}) collective-permute-start(f32[2,384,128]{2,1,0:T(8,128)} %pad_maximum_fusion.8), channel_id=1, source_target_pairs={{1,0},{2,1},{3,2},{5,4},{6,5},{7,6},{9,8},{10,9},{11,10},{13,12},{... | collective-permute-start | bytes 1179656 | tf_op jit(solution)/shard_map/ppermute | solution.py:40
  53.0 27.5 %collective-permute-start.8 = (f32[1,128,384]{2,1,0:T(8,128)}, f32[1,128,384]{2,1,0:T(8,128)}, u32[]{:S(2)}, u32[]{:S(2)}) collective-permute-start(f32[1,128,384]{2,1,0:T(8,128)} %get-tuple-element.355), channel_id=1, source_target_pairs={{4,0},{8,4},{12,8},{16,12},{20,16},{24,20},{28,24},{5,1},{9,5},{13... | collective-permute-start | bytes 589832 | tf_op jit(solution)/shard_map/ppermute | solution.py:27
  54.3 26.2 %collective-permute-start.9 = (f32[1,128,384]{2,1,0:T(8,128)}, f32[1,128,384]{2,1,0:T(8,128)}, u32[]{:S(2)}, u32[]{:S(2)}) collective-permute-start(f32[1,128,384]{2,1,0:T(8,128)} %get-tuple-element.356), channel_id=1, source_target_pairs={{0,4},{4,8},{8,12},{12,16},{16,20},{20,24},{24,28},{1,5},{5,9},{9,... | collective-permute-start | bytes 589832 | tf_op jit(solution)/shard_map/ppermute | solution.py:27
  73.7 61.5 %collective-permute-start.4 = (f32[2,128,384]{2,1,0:T(8,128)}, f32[2,128,384]{2,1,0:T(8,128)}, u32[]{:S(2)}, u32[]{:S(2)}) collective-permute-start(f32[2,128,384]{2,1,0:T(8,128)} %get-tuple-element.353), channel_id=1, source_target_pairs={{4,0},{8,4},{12,8},{16,12},{20,16},{24,20},{28,24},{5,1},{9,5},{13... | collective-permute-start | bytes 1179656 | tf_op jit(solution)/shard_map/ppermute | solution.py:27
  75.0 60.3 %collective-permute-start.5 = (f32[2,128,384]{2,1,0:T(8,128)}, f32[2,128,384]{2,1,0:T(8,128)}, u32[]{:S(2)}, u32[]{:S(2)}) collective-permute-start(f32[2,128,384]{2,1,0:T(8,128)} %get-tuple-element.354), channel_id=1, source_target_pairs={{0,4},{4,8},{8,12},{12,16},{16,20},{20,24},{24,28},{1,5},{5,9},{9,... | collective-permute-start | bytes 1179656 | tf_op jit(solution)/shard_map/ppermute | solution.py:27
  81.7 5.1 collective-permute-start.10
  136.6 5.2 %collective-permute-start.6 = (f32[2,128,128]{2,1,0:T(8,128)S(1)}, f32[2,128,128]{2,1,0:T(8,128)S(1)}, u32[]{:S(2)}, u32[]{:S(2)}) collective-permute-start(f32[2,128,128]{2,1,0:T(8,128)S(1)} %get-tuple-element.368), channel_id=1, source_target_pairs={{1,0},{2,1},{3,2},{5,4},{6,5},{7,6},{9,8},{10,9},{11,10},{13,12},{... | collective-permute-start | bytes 393224 | tf_op jit(solution)/shard_map/ppermute | solution.py:27
  142.8 8.1 %collective-permute-start.12 = (f32[2,128,128]{2,1,0:T(8,128)S(1)}, f32[2,128,128]{2,1,0:T(8,128)S(1)}, u32[]{:S(2)}, u32[]{:S(2)}) collective-permute-start(f32[2,128,128]{2,1,0:T(8,128)S(1)} %fusion.63), channel_id=1, source_target_pairs={{0,4},{4,8},{8,12},{12,16},{16,20},{20,24},{24,28},{1,5},{5,9},{9,... | collective-permute-start | bytes 393224 | tf_op jit(solution)/shard_map/ppermute | solution.py:38
  147.0 8.2 %collective-permute-start.13 = (f32[2,128,128]{2,1,0:T(8,128)S(1)}, f32[2,128,128]{2,1,0:T(8,128)S(1)}, u32[]{:S(2)}, u32[]{:S(2)}) collective-permute-start(f32[2,128,128]{2,1,0:T(8,128)S(1)} %fusion.63), channel_id=1, source_target_pairs={{4,0},{8,4},{12,8},{16,12},{20,16},{24,20},{28,24},{5,1},{9,5},{13... | collective-permute-start | bytes 393224 | tf_op jit(solution)/shard_map/ppermute | solution.py:40
  157.3 5.1 collective-permute-start.15
  180.2 10.6 %collective-permute-start.16 = (f32[2,128,384]{2,1,0:T(8,128)S(1)}, f32[2,128,384]{2,1,0:T(8,128)S(1)}, u32[]{:S(2)}, u32[]{:S(2)}) collective-permute-start(f32[2,128,384]{2,1,0:T(8,128)S(1)} %get-tuple-element.351), channel_id=1, source_target_pairs={{4,0},{8,4},{12,8},{16,12},{20,16},{24,20},{28,24},{5,1},{9,5},{13... | collective-permute-start | bytes 1179656 | tf_op jit(solution)/shard_map/ppermute | solution.py:27
  181.5 21.7 %collective-permute-start.17 = (f32[2,128,384]{2,1,0:T(8,128)S(1)}, f32[2,128,384]{2,1,0:T(8,128)S(1)}, u32[]{:S(2)}, u32[]{:S(2)}) collective-permute-start(f32[2,128,384]{2,1,0:T(8,128)S(1)} %get-tuple-element.352), channel_id=1, source_target_pairs={{0,4},{4,8},{8,12},{12,16},{16,20},{20,24},{24,28},{1,5},{5,9},{9,... | collective-permute-start | bytes 1179656 | tf_op jit(solution)/shard_map/ppermute | solution.py:27
  208.9 6.6 %collective-permute-start.20 = (f32[2,128,128]{2,1,0:T(8,128)S(1)}, f32[2,128,128]{2,1,0:T(8,128)S(1)}, u32[]{:S(2)}, u32[]{:S(2)}) collective-permute-start(f32[2,128,128]{2,1,0:T(8,128)S(1)} %fusion.60), channel_id=1, source_target_pairs={{0,4},{4,8},{8,12},{12,16},{16,20},{20,24},{24,28},{1,5},{5,9},{9,... | collective-permute-start | bytes 393224 | tf_op jit(solution)/shard_map/ppermute | solution.py:38
  213.0 6.9 %collective-permute-start.21 = (f32[2,128,128]{2,1,0:T(8,128)S(1)}, f32[2,128,128]{2,1,0:T(8,128)S(1)}, u32[]{:S(2)}, u32[]{:S(2)}) collective-permute-start(f32[2,128,128]{2,1,0:T(8,128)S(1)} %fusion.60), channel_id=1, source_target_pairs={{4,0},{8,4},{12,8},{16,12},{20,16},{24,20},{28,24},{5,1},{9,5},{13... | collective-permute-start | bytes 393224 | tf_op jit(solution)/shard_map/ppermute | solution.py:40
  223.1 7.2 %collective-permute-start.23 = (f32[2,384,128]{2,1,0:T(8,128)S(1)}, f32[2,384,128]{2,1,0:T(8,128)S(1)}, u32[]{:S(2)}, u32[]{:S(2)}) collective-permute-start(f32[2,384,128]{2,1,0:T(8,128)S(1)} %pad_maximum_fusion.10), channel_id=1, source_target_pairs={{1,0},{2,1},{3,2},{5,4},{6,5},{7,6},{9,8},{10,9},{11,10},{13,12},{... | collective-permute-start | bytes 1179656 | tf_op jit(solution)/shard_map/ppermute | solution.py:40
  245.6 255.9 %all-reduce.5.cloned.1.call-start = ((), (), s32[]{:S(2)}) async-start(), calls=%async_computation.1 | async-start | bytes 8388608 | tf_op jit(solution)/shard_map/psum | solution.py:17
  253.7 161.0 %collective-permute-start.24 = (f32[2,128,384]{2,1,0:T(8,128)}, f32[2,128,384]{2,1,0:T(8,128)}, u32[]{:S(2)}, u32[]{:S(2)}) collective-permute-start(f32[2,128,384]{2,1,0:T(8,128)} %get-tuple-element.349), channel_id=1, source_target_pairs={{4,0},{8,4},{12,8},{16,12},{20,16},{24,20},{28,24},{5,1},{9,5},{13... | collective-permute-start | bytes 1179656 | tf_op jit(solution)/shard_map/ppermute | solution.py:27
  255.0 159.7 %collective-permute-start.25 = (f32[2,128,384]{2,1,0:T(8,128)}, f32[2,128,384]{2,1,0:T(8,128)}, u32[]{:S(2)}, u32[]{:S(2)}) collective-permute-start(f32[2,128,384]{2,1,0:T(8,128)} %get-tuple-element.350), channel_id=1, source_target_pairs={{0,4},{4,8},{8,12},{12,16},{16,20},{20,24},{24,28},{1,5},{5,9},{9,... | collective-permute-start | bytes 1179656 | tf_op jit(solution)/shard_map/ppermute | solution.py:27
  415.9 6.7 %collective-permute-start.26 = (f32[2,128,128]{2,1,0:T(8,128)S(1)}, f32[2,128,128]{2,1,0:T(8,128)S(1)}, u32[]{:S(2)}, u32[]{:S(2)}) collective-permute-start(f32[2,128,128]{2,1,0:T(8,128)S(1)} %get-tuple-element.364), channel_id=1, source_target_pairs={{1,0},{2,1},{3,2},{5,4},{6,5},{7,6},{9,8},{10,9},{11,10},{13,12},{... | collective-permute-start | bytes 393224 | tf_op jit(solution)/shard_map/ppermute | solution.py:27
  417.2 5.4 %collective-permute-start.27 = (f32[2,128,128]{2,1,0:T(8,128)S(1)}, f32[2,128,128]{2,1,0:T(8,128)S(1)}, u32[]{:S(2)}, u32[]{:S(2)}) collective-permute-start(f32[2,128,128]{2,1,0:T(8,128)S(1)} %get-tuple-element.365), channel_id=1, source_target_pairs={{0,1},{1,2},{2,3},{4,5},{5,6},{6,7},{8,9},{9,10},{10,11},{12,13},{... | collective-permute-start | bytes 393224 | tf_op jit(solution)/shard_map/ppermute | solution.py:27
  (36 other events, 247.2 us)
Sparse Core Ops, SparseCore 0:
  245.7 168.8 all-reduce.2
  417.0 84.4 all-reduce.4
